TPU v7x, 256 devices: a whole 4x4x8 slice. The times are simulated.
256 devices in a mesh: grp: 2 (over z_hi), mem: 128 (over x, z_lo, y, core).
Axes of the slice: x: 4, y: 4, z: 8 (z_hi: 2, z_lo: 4; z = z_hi * 4 + z_lo), core: 2. Of those that a mesh axis runs over, the one named last changes fastest.
Arguments:
- state_ens: bfloat16 [512, 131072], P('mem', 'grp'), may hold values from -6 to 6
- obs_ens: bfloat16 [512, 262144], P('mem', 'grp'), may hold values from -6 to 6
- obs_value: float32 [262144], P(('grp', 'mem')), may hold values from -12 to 12
- obs_class: int32 [262144], P(('grp', 'mem')), may hold values from 0 to 15
- loc_table: bfloat16 [16], replicated, may hold values from 0.049804688 to 1
- nbr_weight: float32 [4], replicated, may hold values from 0.25 to 1
Outputs:
- analysis: bfloat16 [512, 131072], P('mem', 'grp')
All inputs are finite; a program needn't handle non-finite values.
Results may differ from a plain program's by a relative error of at most 0.0065.
Values may be sent and summed in bfloat16 or wider, within the bound.
No kernel may reach another device: no remote copies, remote signals or barrier semaphores. Data moves between devices by JAX's collectives and lax.ppermute only.
A program may use at most 64 MiB of HBM per device.

v0:
```python
import jax
import jax.numpy as jnp
from jax import lax
from jax.experimental import pallas as pl
from jax.experimental.pallas import tpu as pltpu
from jax.sharding import PartitionSpec as P

MEMBERS = 512
SWEEPS = 5
ROW_PATCHES = 8
HALF = MEMBERS // 2
VEC = 16
FIRST = MEMBERS + VEC
PACKED = FIRST + HALF + VEC
F32 = jnp.float32
BF16 = jnp.bfloat16


def placement():
    order = []
    for row in range(16):
        z, step = row // 4, row % 4
        x = step if z % 2 == 0 else 3 - step
        order += [x * 32 + z * 8 + w for w in range(ROW_PATCHES)]
    return order


ORDER = placement()


def device_of(patch):
    return patch // 128 * 128 + ORDER[patch % 128]


def links(by):
    pairs = []
    for p in range(256):
        q = p + by
        if 0 <= q < 256 and (abs(by) == ROW_PATCHES or p // ROW_PATCHES == q // ROW_PATCHES):
            pairs.append((device_of(p), device_of(q)))
    return pairs


def lookup(classes, weight_table):
    codes = lax.broadcasted_iota(jnp.int32, (weight_table.shape[0], classes.shape[0]), 0)
    picked = jnp.where(codes == classes[None, :], weight_table.astype(F32)[:, None], 0.0)
    return jnp.sum(picked, axis=0)


def member_sum(ref):
    def step(i, acc):
        return acc + jnp.sum(ref[pl.ds(i * 4, 4)].astype(F32), axis=(0, 1))

    acc = lax.fori_loop(0, 16, step, jnp.zeros((4, ref.shape[3]), F32))
    return jnp.sum(acc, axis=0, keepdims=True)


def rows_of(ref, i):
    block = ref[pl.ds(i * 4, 4)].astype(F32)
    return jnp.concatenate([block[:, 0], block[:, 1]], axis=1).reshape(32, ref.shape[3])


def gram_kernel(obs_ref, val_ref, own_ref, send_ref, spread_ref, left_ref):
    centre = member_sum(obs_ref) / MEMBERS
    observed = val_ref[0:1]
    rates = val_ref[1:2]

    def step(i, carry):
        spread = (rows_of(obs_ref, i) - centre).astype(BF16)
        at = pl.ds(pl.multiple_of(i * 32, 32), 32)
        spread_ref[at] = spread
        left_ref[at] = (spread.astype(F32) * rates).astype(BF16)
        return carry

    lax.fori_loop(0, 16, step, 0)
    innovation = (rates * (observed - centre)).astype(BF16)
    left_ref[pl.ds(MEMBERS, VEC)] = jnp.broadcast_to(innovation, (VEC, innovation.shape[1]))
    contract = (((1,), (1,)), ((), ()))
    is_first = lax.broadcasted_iota(jnp.int32, (VEC, HALF), 0) < 8
    for start, rows, at in ((0, FIRST, 0), (HALF, FIRST - HALF, FIRST)):
        part = lax.dot_general(
            left_ref[pl.ds(start, rows)],
            spread_ref[pl.ds(start, HALF)],
            contract,
            preferred_element_type=F32,
        )
        body = rows - VEC
        own_ref[pl.ds(at, body)] = part[:body]
        send_ref[pl.ds(at, body)] = part[:body].astype(BF16)
        vec = part[body:]
        high = vec.astype(BF16)
        low = (vec - high.astype(F32)).astype(BF16)
        own_ref[pl.ds(at + body, VEC)] = jnp.where(is_first, vec, 0.0)
        send_ref[pl.ds(at + body, VEC)] = jnp.where(
            is_first, high.astype(F32), low.astype(F32)
        ).astype(BF16)


def solve_kernel(
    weight_ref, own_ref, west_ref, east_ref, north_ref, south_ref, out_ref,
    sys_ref, t_ref, w_ref, t2_ref, tb_ref, wb_ref, t2b_ref,
):
    def total(start, rows):
        at = pl.ds(start, rows)
        acc = own_ref[at]
        for k, ref in enumerate((west_ref, east_ref, north_ref, south_ref)):
            acc = acc + weight_ref[k] * ref[at].astype(F32)
        return acc

    row = lax.broadcasted_iota(jnp.int32, (HALF, HALF), 0)
    col = lax.broadcasted_iota(jnp.int32, (HALF, HALF), 1)

    def mirrored(block):
        block = jnp.where(row >= col, block, block.T)
        return block + jnp.where(row == col, MEMBERS - 1.0, 0.0)

    sys_ref[0:HALF, 0:HALF] = mirrored(total(0, HALF))
    cross = total(HALF, HALF)
    sys_ref[HALF:MEMBERS, 0:HALF] = cross
    sys_ref[0:HALF, HALF:MEMBERS] = cross.T
    sys_ref[HALF:MEMBERS, HALF:MEMBERS] = mirrored(total(FIRST, HALF))
    vec0 = total(MEMBERS, VEC)
    vec1 = total(FIRST + HALF, VEC)
    rhs = jnp.concatenate([vec0[0:1] + vec0[8:9], vec1[0:1] + vec1[8:9]], axis=1)

    system = sys_ref[...]
    norm = jnp.sqrt(jnp.sum(jnp.sum(system * system, axis=0, keepdims=True), axis=1, keepdims=True))
    t = system / norm
    t_ref[...] = t
    tb_ref[...] = t.astype(BF16)

    def dot(a, b):
        return jnp.dot(a[...], b[...], preferred_element_type=F32)

    scale = 1.0
    for sweep in range(SWEEPS):
        last = sweep == SWEEPS - 1
        if sweep == 0:
            w = -0.5 * t_ref[...]
        else:
            w = 1.5 * w_ref[...] - (0.5 * scale) * t_ref[...] - 0.5 * dot(tb_ref, wb_ref)
        scale *= 1.5
        w_ref[...] = w
        if not last:
            wb_ref[...] = w.astype(BF16)
            t2 = dot(tb_ref, tb_ref)
            t2_ref[...] = t2
            t2b_ref[...] = t2.astype(BF16)
            t = 2.25 * t_ref[...] - 1.5 * t2_ref[...] + 0.25 * dot(t2b_ref, tb_ref)
            t_ref[...] = t
            tb_ref[...] = t.astype(BF16)

    row = lax.broadcasted_iota(jnp.int32, (MEMBERS, MEMBERS), 0)
    col = lax.broadcasted_iota(jnp.int32, (MEMBERS, MEMBERS), 1)
    root_inv = w_ref[...] + jnp.where(row == col, scale, 0.0)
    half_step = jnp.sum(root_inv * rhs, axis=1, keepdims=True)
    mean_weight = jnp.sum(root_inv * half_step, axis=0, keepdims=True) / norm
    out_ref[...] = (jnp.sqrt((MEMBERS - 1.0) / norm) * root_inv + mean_weight).astype(BF16)


def update_kernel(transform_ref, state_ref, out_ref, dev_ref):
    centre = member_sum(state_ref) / MEMBERS

    def step(i, carry):
        at = pl.ds(pl.multiple_of(i * 32, 32), 32)
        dev_ref[at] = (rows_of(state_ref, i) - centre).astype(BF16)
        return carry

    lax.fori_loop(0, 16, step, 0)
    update = jnp.dot(transform_ref[...], dev_ref[...], preferred_element_type=F32)
    analysis = (centre + update).reshape(64, 8, centre.shape[1])
    out_ref[:, 0] = analysis[:, 0:4].astype(BF16)
    out_ref[:, 1] = analysis[:, 4:8].astype(BF16)


VMEM = pl.BlockSpec(memory_space=pltpu.VMEM)
SMEM = pl.BlockSpec(memory_space=pltpu.SMEM)


def to_patches(array, columns):
    pieces = lax.all_to_all(
        array.reshape(4, 128, columns), "mem", split_axis=1, concat_axis=0, tiled=False,
        axis_index_groups=[ORDER],
    )
    return pieces.reshape(64, 2, 4, columns)


def shards(state_ens, obs_ens, obs_value, obs_class, loc_table, nbr_weight):
    obs = to_patches(obs_ens, 1024)
    values = jnp.stack([obs_value, lookup(obs_class, loc_table)])
    values = lax.ppermute(values, ("grp", "mem"), [(p, device_of(p)) for p in range(256)])
    state_ens, obs, values = lax.optimization_barrier((state_ens, obs, values))
    state = to_patches(state_ens, 512)
    own, send = pl.pallas_call(
        gram_kernel,
        out_shape=(
            jax.ShapeDtypeStruct((PACKED, HALF), F32),
            jax.ShapeDtypeStruct((PACKED, HALF), BF16),
        ),
        in_specs=[VMEM, VMEM],
        out_specs=(VMEM, VMEM),
        scratch_shapes=[pltpu.VMEM((MEMBERS, 1024), BF16), pltpu.VMEM((FIRST, 1024), BF16)],
        name="gram",
    )(obs, values)
    north, south = (lax.ppermute(send, ("grp", "mem"), links(by)) for by in (8, -8))
    west, east = (lax.ppermute(send, ("grp", "mem"), links(by)) for by in (1, -1))
    square = (MEMBERS, MEMBERS)
    transform = pl.pallas_call(
        solve_kernel,
        out_shape=jax.ShapeDtypeStruct(square, BF16),
        in_specs=[SMEM] + [VMEM] * 5,
        out_specs=VMEM,
        scratch_shapes=[pltpu.VMEM(square, F32)] * 4 + [pltpu.VMEM(square, BF16)] * 3,
        name="solve",
    )(nbr_weight, own, west, east, north, south)
    analysis = pl.pallas_call(
        update_kernel,
        out_shape=jax.ShapeDtypeStruct((64, 2, 4, 512), BF16),
        in_specs=[VMEM, VMEM],
        out_specs=VMEM,
        scratch_shapes=[pltpu.VMEM(square, BF16)],
        name="update",
    )(transform, state)
    back = lax.all_to_all(
        analysis.reshape(128, 4, 512), "mem", split_axis=0, concat_axis=1, tiled=False,
        axis_index_groups=[ORDER],
    )
    return back.reshape(4, 65536)


def solution(mesh):
    in_specs = (P("mem", "grp"), P("mem", "grp"), P(("grp", "mem")), P(("grp", "mem")), P(), P())
    out_specs = P("mem", "grp")
    return jax.shard_map(shards, mesh=mesh, in_specs=in_specs, out_specs=out_specs, check_vma=False)
```

profile of v0, /device:TPU:1, one launch (start us, length us, event | category | flops | bytes accessed | tf_op | source)
XLA Modules:
  0.0 117.4 jit_solution(434487680589427774)
XLA Ops:
  0.0 0.0 copy-start.9
  0.0 0.0 copy-start.7
  0.0 14.0 %all-to-all-start = ((bf16[1,4,128,1024]{3,1,0,2:T(4,128)(2,1)}), bf16[1,4,128,1024]{3,1,0,2:T(4,128)(2,1)S(1)}, u32[]{:S(2)}, u32[]{:S(2)}) async-start(bf16[1,4,128,1024]{3,1,0,2:T(4,128)(2,1)} %bitcast.26), calls=%async_computation | async-start | bytes 2097152 | tf_op jit(solution)/shard_map/all_to_all | solution.py:181
  14.0 0.0 copy-done.9
  14.0 0.0 copy-done.7
  14.0 0.0 copy-start.8
  14.0 0.1 select_reduce_fusion
  14.1 0.6 copy-done.8
  14.7 0.7 collective-permute-start
  15.4 0.0 collective-permute-done.val_ref
  15.4 0.0 copy-start.6
  15.4 28.0 %all-to-all-done = bf16[1,4,128,1024]{3,1,0,2:T(4,128)(2,1)S(1)} async-done(((bf16[1,4,128,1024]{3,1,0,2:T(4,128)(2,1)}), bf16[1,4,128,1024]{3,1,0,2:T(4,128)(2,1)S(1)}, u32[]{:S(2)}, u32[]{:S(2)}) %all-to-all-start) | async-done | bytes 1048608 | tf_op jit(solution)/shard_map/all_to_all | solution.py:181
  43.4 0.0 copy-start
  43.4 0.0 copy-done.6
  43.4 6.8 %all-to-all-start.1 = ((bf16[1,4,128,512]{3,1,0,2:T(4,128)(2,1)}), bf16[1,4,128,512]{3,1,0,2:T(4,128)(2,1)S(1)}, u32[]{:S(2)}, u32[]{:S(2)}) async-start(bf16[1,4,128,512]{3,1,0,2:T(4,128)(2,1)} %bitcast.6), calls=%async_computation.1 | async-start | bytes 1048576 | tf_op jit(solution)/shard_map/all_to_all | solution.py:181
  50.2 0.0 copy-done
  50.2 4.0 %gram.1 = (f32[800,256]{1,0:T(8,128)}, bf16[800,256]{1,0:T(8,128)(2,1)}) custom-call(bf16[64,2,4,1024]{3,2,1,0:T(4,128)(2,1)} %bitcast.22, f32[2,1024]{1,0:T(2,128)} %copy-done.6), custom_call_target="tpu_custom_call" | custom-call | tf_op jit(solution)/shard_map/gram/pallas_call | solution.py:194
  54.2 3.5 %collective-permute-start.1 = (bf16[800,256]{1,0:T(8,128)(2,1)}, bf16[800,256]{1,0:T(8,128)(2,1)S(1)}, u32[]{:S(2)}, u32[]{:S(2)}) collective-permute-start(bf16[800,256]{1,0:T(8,128)(2,1)} %get-tuple-element.13), channel_id=1, source_target_pairs={{0,1},{1,2},{2,3},{3,4},{4,5},{5,6},{6,7},{32,33},{33,34},{34,35},... | collective-permute-start | bytes 1228808 | tf_op jit(solution)/shard_map/ppermute | solution.py:206
  57.7 1.9 %collective-permute-start.2 = (bf16[800,256]{1,0:T(8,128)(2,1)}, bf16[800,256]{1,0:T(8,128)(2,1)S(1)}, u32[]{:S(2)}, u32[]{:S(2)}) collective-permute-start(bf16[800,256]{1,0:T(8,128)(2,1)} %get-tuple-element.13), channel_id=1, source_target_pairs={{1,0},{2,1},{3,2},{4,3},{5,4},{6,5},{7,6},{33,32},{34,33},{35,34},... | collective-permute-start | bytes 1228808 | tf_op jit(solution)/shard_map/ppermute | solution.py:206
  59.6 3.1 %collective-permute-start.3 = (bf16[800,256]{1,0:T(8,128)(2,1)}, bf16[800,256]{1,0:T(8,128)(2,1)S(1)}, u32[]{:S(2)}, u32[]{:S(2)}) collective-permute-start(bf16[800,256]{1,0:T(8,128)(2,1)} %get-tuple-element.13), channel_id=1, source_target_pairs={{0,32},{1,33},{2,34},{3,35},{4,36},{5,37},{6,38},{7,39},{32,64},{3... | collective-permute-start | bytes 1228808 | tf_op jit(solution)/shard_map/ppermute | solution.py:205
  62.8 1.3 %collective-permute-start.4 = (bf16[800,256]{1,0:T(8,128)(2,1)}, bf16[800,256]{1,0:T(8,128)(2,1)S(1)}, u32[]{:S(2)}, u32[]{:S(2)}) collective-permute-start(bf16[800,256]{1,0:T(8,128)(2,1)} %get-tuple-element.13), channel_id=1, source_target_pairs={{32,0},{33,1},{34,2},{35,3},{36,4},{37,5},{38,6},{39,7},{64,32},{6... | collective-permute-start | bytes 1228808 | tf_op jit(solution)/shard_map/ppermute | solution.py:205
  64.1 0.0 collective-permute-done.1.west_ref
  64.1 0.0 copy-start.2
  64.1 4.3 %collective-permute-done.2.east_ref = bf16[800,256]{1,0:T(8,128)(2,1)S(1)} collective-permute-done((bf16[800,256]{1,0:T(8,128)(2,1)}, bf16[800,256]{1,0:T(8,128)(2,1)S(1)}, u32[]{:S(2)}, u32[]{:S(2)}) %collective-permute-start.2) | collective-permute-done | bytes 409632 | tf_op jit(solution)/shard_map/ppermute | solution.py:206
  68.4 0.0 copy-start.3
  68.4 3.1 %collective-permute-done.3.north_ref = bf16[800,256]{1,0:T(8,128)(2,1)S(1)} collective-permute-done((bf16[800,256]{1,0:T(8,128)(2,1)}, bf16[800,256]{1,0:T(8,128)(2,1)S(1)}, u32[]{:S(2)}, u32[]{:S(2)}) %collective-permute-start.3) | collective-permute-done | bytes 409632 | tf_op jit(solution)/shard_map/ppermute | solution.py:205
  71.5 0.0 copy-start.4
  71.5 3.8 %collective-permute-done.4.south_ref = bf16[800,256]{1,0:T(8,128)(2,1)S(1)} collective-permute-done((bf16[800,256]{1,0:T(8,128)(2,1)}, bf16[800,256]{1,0:T(8,128)(2,1)S(1)}, u32[]{:S(2)}, u32[]{:S(2)}) %collective-permute-start.4) | collective-permute-done | bytes 409632 | tf_op jit(solution)/shard_map/ppermute | solution.py:205
  75.2 0.0 copy-start.5
  75.2 0.0 copy-done.2
  75.2 0.0 copy-done.3
  75.2 0.0 copy-done.4
  75.2 0.7 copy-done.5
  76.0 7.0 %solve.1.transform_ref = bf16[512,512]{1,0:T(8,128)(2,1)} custom-call(f32[4]{0:T(128)} %weight_ref.1, f32[800,256]{1,0:T(8,128)} %get-tuple-element.12.own_ref, bf16[800,256]{1,0:T(8,128)(2,1)} %copy-done.2, bf16[800,256]{1,0:T(8,128)(2,1)} %copy-done.3, bf16[800,256]{1,0:T(8,128)(2,1)} %copy-done.4, bf16[800,256]{1,0:T(8,128)(2,1)} %copy-done.5), custom_call_target="tpu_custom_call" | custom-call | tf_op jit(solution)/shard_map/solve/pallas_call | solution.py:208
  82.9 0.0 all-to-all-done.1
  82.9 0.0 copy-start.1
  83.0 0.8 copy-done.1
  83.7 3.0 %update.1 = bf16[64,2,4,512]{3,2,1,0:T(4,128)(2,1)} custom-call(bf16[512,512]{1,0:T(8,128)(2,1)} %solve.1.transform_ref, bf16[64,2,4,512]{3,2,1,0:T(4,128)(2,1)} %bitcast.23), custom_call_target="tpu_custom_call" | custom-call | tf_op jit(solution)/shard_map/update/pallas_call | solution.py:216
  86.7 29.8 %all_to_all.45 = bf16[128,4,1,512]{3,1,2,0:T(4,128)(2,1)S(1)} all-to-all(bf16[128,4,1,512]{3,1,2,0:T(4,128)(2,1)} %bitcast.24), channel_id=1, replica_groups={{0,1,2,3,4,5,6,7,32,33,34,35,36,37,38,39,64,65,66,67,68,69,70,71,96,97,..., dimensions={0} | all-to-all | bytes 1048576 | tf_op jit(solution)/shard_map/all_to_all | solution.py:224
  116.6 0.8 copy.13
  (2 shorter events, 0.0 us)
Async XLA Ops:
  0.0 14.0 %copy-start.9 = (bf16[16]{0:T(256)(128)(2,1)S(1)}, bf16[16]{0:T(256)(128)(2,1)}, u32[]{:S(2)}) copy-start(bf16[16]{0:T(256)(128)(2,1)} %param.10) | copy-start | bytes 100
  0.0 14.0 %copy-start.7 = (s32[1024]{0:T(1024)S(1)}, s32[1024]{0:T(1024)}, u32[]{:S(2)}) copy-start(s32[1024]{0:T(1024)} %param.9) | copy-start | bytes 12292
  0.0 43.4 %all-to-all-start = ((bf16[1,4,128,1024]{3,1,0,2:T(4,128)(2,1)}), bf16[1,4,128,1024]{3,1,0,2:T(4,128)(2,1)S(1)}, u32[]{:S(2)}, u32[]{:S(2)}) async-start(bf16[1,4,128,1024]{3,1,0,2:T(4,128)(2,1)} %bitcast.26), calls=%async_computation | async-start | bytes 2097152 | tf_op jit(solution)/shard_map/all_to_all | solution.py:181
  14.0 0.7 copy-start.8
  14.7 0.7 collective-permute-start
  15.4 28.0 %copy-start.6 = (f32[2,1024]{1,0:T(2,128)}, f32[2,1024]{1,0:T(2,128)S(1)}, u32[]{:S(2)}) copy-start(f32[2,1024]{1,0:T(2,128)S(1)} %collective-permute-done.val_ref) | copy-start | bytes 24580
  43.4 6.8 %copy-start = (bf16[1,4,128,1024]{3,1,0,2:T(4,128)(2,1)}, bf16[1,4,128,1024]{3,1,0,2:T(4,128)(2,1)S(1)}, u32[]{:S(2)}) copy-start(bf16[1,4,128,1024]{3,1,0,2:T(4,128)(2,1)S(1)} %all-to-all-done) | copy-start | bytes 3145732
  43.4 39.6 %all-to-all-start.1 = ((bf16[1,4,128,512]{3,1,0,2:T(4,128)(2,1)}), bf16[1,4,128,512]{3,1,0,2:T(4,128)(2,1)S(1)}, u32[]{:S(2)}, u32[]{:S(2)}) async-start(bf16[1,4,128,512]{3,1,0,2:T(4,128)(2,1)} %bitcast.6), calls=%async_computation.1 | async-start | bytes 1048576 | tf_op jit(solution)/shard_map/all_to_all | solution.py:181
  54.2 9.9 %collective-permute-start.1 = (bf16[800,256]{1,0:T(8,128)(2,1)}, bf16[800,256]{1,0:T(8,128)(2,1)S(1)}, u32[]{:S(2)}, u32[]{:S(2)}) collective-permute-start(bf16[800,256]{1,0:T(8,128)(2,1)} %get-tuple-element.13), channel_id=1, source_target_pairs={{0,1},{1,2},{2,3},{3,4},{4,5},{5,6},{6,7},{32,33},{33,34},{34,35},... | collective-permute-start | bytes 1228808 | tf_op jit(solution)/shard_map/ppermute | solution.py:206
  57.7 10.7 %collective-permute-start.2 = (bf16[800,256]{1,0:T(8,128)(2,1)}, bf16[800,256]{1,0:T(8,128)(2,1)S(1)}, u32[]{:S(2)}, u32[]{:S(2)}) collective-permute-start(bf16[800,256]{1,0:T(8,128)(2,1)} %get-tuple-element.13), channel_id=1, source_target_pairs={{1,0},{2,1},{3,2},{4,3},{5,4},{6,5},{7,6},{33,32},{34,33},{35,34},... | collective-permute-start | bytes 1228808 | tf_op jit(solution)/shard_map/ppermute | solution.py:206
  59.6 11.8 %collective-permute-start.3 = (bf16[800,256]{1,0:T(8,128)(2,1)}, bf16[800,256]{1,0:T(8,128)(2,1)S(1)}, u32[]{:S(2)}, u32[]{:S(2)}) collective-permute-start(bf16[800,256]{1,0:T(8,128)(2,1)} %get-tuple-element.13), channel_id=1, source_target_pairs={{0,32},{1,33},{2,34},{3,35},{4,36},{5,37},{6,38},{7,39},{32,64},{3... | collective-permute-start | bytes 1228808 | tf_op jit(solution)/shard_map/ppermute | solution.py:205
  62.8 12.5 %collective-permute-start.4 = (bf16[800,256]{1,0:T(8,128)(2,1)}, bf16[800,256]{1,0:T(8,128)(2,1)S(1)}, u32[]{:S(2)}, u32[]{:S(2)}) collective-permute-start(bf16[800,256]{1,0:T(8,128)(2,1)} %get-tuple-element.13), channel_id=1, source_target_pairs={{32,0},{33,1},{34,2},{35,3},{36,4},{37,5},{38,6},{39,7},{64,32},{6... | collective-permute-start | bytes 1228808 | tf_op jit(solution)/shard_map/ppermute | solution.py:205
  64.1 11.2 %copy-start.2 = (bf16[800,256]{1,0:T(8,128)(2,1)}, bf16[800,256]{1,0:T(8,128)(2,1)S(1)}, u32[]{:S(2)}) copy-start(bf16[800,256]{1,0:T(8,128)(2,1)S(1)} %collective-permute-done.1.west_ref) | copy-start | bytes 1228804
  68.4 6.8 %copy-start.3 = (bf16[800,256]{1,0:T(8,128)(2,1)}, bf16[800,256]{1,0:T(8,128)(2,1)S(1)}, u32[]{:S(2)}) copy-start(bf16[800,256]{1,0:T(8,128)(2,1)S(1)} %collective-permute-done.2.east_ref) | copy-start | bytes 1228804
  71.5 3.8 %copy-start.4 = (bf16[800,256]{1,0:T(8,128)(2,1)}, bf16[800,256]{1,0:T(8,128)(2,1)S(1)}, u32[]{:S(2)}) copy-start(bf16[800,256]{1,0:T(8,128)(2,1)S(1)} %collective-permute-done.3.north_ref) | copy-start | bytes 1228804
  75.2 0.7 copy-start.5
  82.9 0.8 copy-start.1
where the time goes:
time: 118 us; the launch traced here: 117 us
  waiting for transfers between devices  39.2 us (33%)
  starting transfers between devices  31.3 us (27%)
  blocking collectives  29.8 us (25%)
  Pallas kernels  13.9 us (12%)
  local copies, waits for them, and re-layouts  2.94 us (2%)
    all_to_all x1, blocking collectives, shards(): lax.all_to_all(analysis.reshape(128, 4, 512), 'mem', split_axis=0, concat...  29.8 us
    all_to_all x2, waiting for transfers between devices, to_patches(): lax.all_to_all(array.reshape(4, 128, columns), 'mem', split_axis=1, conca...  28 us
    all_to_all x2, starting transfers between devices, to_patches(): lax.all_to_all(array.reshape(4, 128, columns), 'mem', split_axis=1, conca...  20.7 us
    ppermute x4, waiting for transfers between devices, shards(): lax.ppermute(send, ('grp', 'mem'), links(by))  11.2 us
    ppermute x4, starting transfers between devices, shards(): lax.ppermute(send, ('grp', 'mem'), links(by))  9.86 us
    pallas_call x1, Pallas kernels, shards(): pl.pallas_call(solve_kernel, out_shape=jax.ShapeDtypeStruct(square, BF16)...  6.97 us
    pallas_call x1, Pallas kernels, shards(): pl.pallas_call(gram_kernel, out_shape=(jax.ShapeDtypeStruct((PACKED, HALF...  3.97 us
    pallas_call x1, Pallas kernels, shards(): pl.pallas_call(update_kernel, out_shape=jax.ShapeDtypeStruct((64, 2, 4, 5...  2.99 us
  transfers between devices with their start and end apart: 7, of which 4 were waited for; matrix products, arithmetic and copies ran while one was open for 0% of the time, Pallas kernels for 9%

commit v1 on v0

v1 whole, which is shorter than its diff:
```python
import jax
import jax.numpy as jnp
from jax import lax
from jax.experimental import pallas as pl
from jax.experimental.pallas import tpu as pltpu
from jax.sharding import PartitionSpec as P

MEMBERS = 512
SWEEPS = 5
CELLS = 512
LOCAL_OBS = 1024
ROW_PATCHES = 8
HALF = MEMBERS // 2
QUARTER = MEMBERS // 4
VEC = 16
TAIL = MEMBERS + QUARTER
PACKED = TAIL + VEC
F32 = jnp.float32
BF16 = jnp.bfloat16


def placement():
    order = []
    for row in range(16):
        z, step = row // 4, row % 4
        x = step if z % 2 == 0 else 3 - step
        order += [x * 32 + z * 8 + w for w in range(ROW_PATCHES)]
    return order


ORDER = placement()


def device_of(patch):
    return patch // 128 * 128 + ORDER[patch % 128]


def swaps(by, parity):
    pairs = []
    for p in range(256):
        row, column = p // ROW_PATCHES, p % ROW_PATCHES
        q = p + by
        if q < 256 and (by == ROW_PATCHES or q // ROW_PATCHES == row):
            if (row if by == ROW_PATCHES else column) % 2 == parity:
                pairs += [(device_of(p), device_of(q)), (device_of(q), device_of(p))]
    return pairs


def swap_weights(weight_ref):
    west, east, north, south = (weight_ref[k] for k in range(4))
    mem = lax.axis_index("mem")
    even_row = lax.rem(lax.div(mem, 32) + lax.div(mem, 8), 2) == 0
    even_column = lax.rem(mem, 2) == 0
    return (
        jnp.where(even_row, south, north),
        jnp.where(even_row, north, south),
        jnp.where(even_column, west, east),
        jnp.where(even_column, east, west),
    )


def lookup(classes, weight_table):
    codes = lax.broadcasted_iota(jnp.int32, (weight_table.shape[0], classes.shape[0]), 0)
    picked = jnp.where(codes == classes[None, :], weight_table.astype(F32)[:, None], 0.0)
    return jnp.sum(picked, axis=0)


def join_kernel(obs_ref, state_ref, out_ref, sem):
    copies = [
        pltpu.make_async_copy(obs_ref, out_ref.at[:, :, pl.ds(0, LOCAL_OBS)], sem.at[0]),
        pltpu.make_async_copy(state_ref, out_ref.at[:, :, pl.ds(LOCAL_OBS, CELLS)], sem.at[1]),
    ]
    for copy in copies:
        copy.start()
    for copy in copies:
        copy.wait()


def gather_rows(ref, columns, rows_ref):
    width = rows_ref.shape[1]

    def step(i, acc):
        block = ref[pl.ds(i * 4, 4), :, :, columns].astype(F32)
        block = jnp.concatenate([block[:, 0], block[:, 1]], axis=1)
        rows_ref[pl.ds(pl.multiple_of(i * 32, 32), 32)] = block.reshape(32, width).astype(BF16)
        return acc + jnp.sum(block, axis=0)

    acc = lax.fori_loop(0, 16, step, jnp.zeros((8, width), F32))
    return jnp.sum(acc, axis=0, keepdims=True) / MEMBERS


def gram_kernel(obs_ref, val_ref, own_ref, send_ref, spread_ref, left_ref):
    centre = gather_rows(obs_ref, pl.ds(0, LOCAL_OBS), spread_ref)
    observed = val_ref[0:1]
    rates = val_ref[1:2]

    def step(i, carry):
        at = pl.ds(pl.multiple_of(i * 32, 32), 32)
        spread = (spread_ref[at].astype(F32) - centre).astype(BF16)
        spread_ref[at] = spread
        left_ref[at] = (spread.astype(F32) * rates).astype(BF16)
        return carry

    lax.fori_loop(0, 16, step, 0)
    innovation = (rates * (observed - centre)).astype(BF16)
    left_ref[pl.ds(MEMBERS, VEC)] = jnp.broadcast_to(innovation, (VEC, innovation.shape[1]))
    contract = (((1,), (1,)), ((), ()))
    first = lax.dot_general(
        left_ref[...], spread_ref[0:HALF], contract, preferred_element_type=F32
    )
    second = lax.dot_general(
        left_ref[HALF:], spread_ref[HALF:MEMBERS], contract, preferred_element_type=F32
    )
    for at, part in (
        ((slice(0, QUARTER), slice(0, QUARTER)), first[0:QUARTER, 0:QUARTER]),
        ((slice(0, QUARTER), slice(QUARTER, HALF)), second[0:QUARTER, 0:QUARTER]),
        ((slice(QUARTER, MEMBERS), slice(0, HALF)), first[QUARTER:MEMBERS]),
        ((slice(MEMBERS, TAIL), slice(0, HALF)), second[QUARTER:HALF]),
    ):
        own_ref[at] = part
        send_ref[at] = part.astype(BF16)
    row = lax.broadcasted_iota(jnp.int32, (VEC, HALF), 0)
    vec = jnp.where(row < 8, first[MEMBERS:], second[HALF:])
    high = vec.astype(BF16).astype(F32)
    is_high = row % 8 < 4
    own_ref[TAIL:PACKED] = jnp.where(is_high, vec, 0.0)
    send_ref[TAIL:PACKED] = jnp.where(is_high, high, vec - high).astype(BF16)


def solve_kernel(
    weight_ref, own_ref, ns0_ref, ns1_ref, ew1_ref, ew0_ref, dev_ref, centre_ref, out_ref,
    sys_ref, t_ref, w_ref, t2_ref, tb_ref, wb_ref, t2b_ref,
):
    weights = swap_weights(weight_ref)

    def total(start, rows):
        at = pl.ds(start, rows)
        acc = own_ref[at]
        for k, ref in enumerate((ns0_ref, ns1_ref, ew1_ref, ew0_ref)):
            acc = acc + weights[k] * ref[at].astype(F32)
        return acc

    row = lax.broadcasted_iota(jnp.int32, (QUARTER, QUARTER), 0)
    col = lax.broadcasted_iota(jnp.int32, (QUARTER, QUARTER), 1)

    def diagonal(block):
        block = jnp.where(row >= col, block, block.T)
        return block + jnp.where(row == col, MEMBERS - 1.0, 0.0)

    top = total(0, QUARTER)
    for start, left, at in ((0, 0, QUARTER), (HALF, QUARTER, MEMBERS)):
        a, b, c = start, start + QUARTER, start + HALF
        low = total(at, QUARTER)
        sys_ref[a:b, a:b] = diagonal(top[:, left:left + QUARTER])
        sys_ref[b:c, a:b] = low[:, 0:QUARTER]
        sys_ref[a:b, b:c] = low[:, 0:QUARTER].T
        sys_ref[b:c, b:c] = diagonal(low[:, QUARTER:])
    cross = total(HALF, HALF)
    sys_ref[HALF:MEMBERS, 0:HALF] = cross
    sys_ref[0:HALF, HALF:MEMBERS] = cross.T
    vec = total(TAIL, VEC)
    rhs = jnp.concatenate([vec[0:1] + vec[4:5], vec[8:9] + vec[12:13]], axis=1)

    system = sys_ref[...]
    norm = jnp.sqrt(jnp.sum(jnp.sum(system * system, axis=0, keepdims=True), axis=1, keepdims=True))
    t = system / norm
    t_ref[...] = t
    tb_ref[...] = t.astype(BF16)

    def dot(a, b):
        return jnp.dot(a[...], b[...], preferred_element_type=F32)

    scale = 1.0
    for sweep in range(SWEEPS):
        last = sweep == SWEEPS - 1
        if sweep == 0:
            w = -0.5 * t_ref[...]
        else:
            w = 1.5 * w_ref[...] - (0.5 * scale) * t_ref[...] - 0.5 * dot(tb_ref, wb_ref)
        scale *= 1.5
        w_ref[...] = w
        if not last:
            wb_ref[...] = w.astype(BF16)
            t2 = dot(tb_ref, tb_ref)
            t2_ref[...] = t2
            t2b_ref[...] = t2.astype(BF16)
            t = 2.25 * t_ref[...] - 1.5 * t2_ref[...] + 0.25 * dot(t2b_ref, tb_ref)
            t_ref[...] = t
            tb_ref[...] = t.astype(BF16)

    row = lax.broadcasted_iota(jnp.int32, (MEMBERS, MEMBERS), 0)
    col = lax.broadcasted_iota(jnp.int32, (MEMBERS, MEMBERS), 1)
    root_inv = w_ref[...] + jnp.where(row == col, scale, 0.0)
    half_step = jnp.sum(root_inv * rhs, axis=1, keepdims=True)
    mean_weight = jnp.sum(root_inv * half_step, axis=0, keepdims=True) / norm
    tb_ref[...] = (jnp.sqrt((MEMBERS - 1.0) / norm) * root_inv + mean_weight).astype(BF16)
    analysis = (centre_ref[...] + dot(tb_ref, dev_ref)).reshape(64, 8, CELLS)
    out_ref[:, 0] = analysis[:, 0:4].astype(BF16)
    out_ref[:, 1] = analysis[:, 4:8].astype(BF16)


def state_kernel(state_ref, dev_ref, centre_ref):
    centre = gather_rows(state_ref, pl.ds(LOCAL_OBS, CELLS), dev_ref)
    centre_ref[...] = centre

    def step(i, carry):
        at = pl.ds(pl.multiple_of(i * 32, 32), 32)
        dev_ref[at] = (dev_ref[at].astype(F32) - centre).astype(BF16)
        return carry

    lax.fori_loop(0, 16, step, 0)


def vmem(mebibytes):
    return pltpu.CompilerParams(vmem_limit_bytes=mebibytes * 2**20)


VMEM = pl.BlockSpec(memory_space=pltpu.VMEM)
HBM = pl.BlockSpec(memory_space=pltpu.HBM)
SMEM = pl.BlockSpec(memory_space=pltpu.SMEM)


def in_hbm(array):
    return pltpu.with_memory_space_constraint(array, pltpu.HBM)


def shards(state_ens, obs_ens, obs_value, obs_class, loc_table, nbr_weight):
    columns = LOCAL_OBS + CELLS
    both = pl.pallas_call(
        join_kernel,
        out_shape=pltpu.VMEM((128, 4, columns), BF16),
        in_specs=[HBM, HBM],
        out_specs=VMEM,
        scratch_shapes=[pltpu.SemaphoreType.DMA((2,))],
        compiler_params=vmem(2),
        name="join",
    )(
        in_hbm(obs_ens.reshape(4, 128, LOCAL_OBS).transpose(1, 0, 2)),
        in_hbm(state_ens.reshape(4, 128, CELLS).transpose(1, 0, 2)),
    )
    both = lax.all_to_all(
        both, "mem", split_axis=0, concat_axis=0, tiled=False, axis_index_groups=[ORDER]
    ).reshape(64, 2, 4, columns)
    values = jnp.stack([obs_value, lookup(obs_class, loc_table)])
    values = lax.ppermute(values, ("grp", "mem"), [(p, device_of(p)) for p in range(256)])
    own, send = pl.pallas_call(
        gram_kernel,
        out_shape=(
            pltpu.VMEM((PACKED, HALF), F32),
            pltpu.VMEM((PACKED, HALF), BF16),
        ),
        in_specs=[VMEM, VMEM],
        out_specs=(VMEM, VMEM),
        scratch_shapes=[pltpu.VMEM((MEMBERS, LOCAL_OBS), BF16), pltpu.VMEM((MEMBERS + VEC, LOCAL_OBS), BF16)],
        compiler_params=vmem(10),
        name="gram",
    )(both, values)
    received = [
        lax.ppermute(send, ("grp", "mem"), swaps(by, parity))
        for by, parity in ((ROW_PATCHES, 0), (ROW_PATCHES, 1), (1, 1), (1, 0))
    ]
    both, own = lax.optimization_barrier((both, own))
    deviation, centre = pl.pallas_call(
        state_kernel,
        out_shape=(
            jax.ShapeDtypeStruct((MEMBERS, CELLS), BF16),
            jax.ShapeDtypeStruct((1, CELLS), F32),
        ),
        in_specs=[VMEM],
        out_specs=(VMEM, VMEM),
        cost_estimate=pl.CostEstimate(flops=2**20, bytes_accessed=2**21, transcendentals=0),
        compiler_params=vmem(4),
        name="state",
    )(both)
    square = (MEMBERS, MEMBERS)
    analysis = pl.pallas_call(
        solve_kernel,
        out_shape=jax.ShapeDtypeStruct((64, 2, 4, CELLS), BF16),
        in_specs=[SMEM] + [VMEM] * 7,
        out_specs=VMEM,
        scratch_shapes=[pltpu.VMEM(square, F32)] * 4 + [pltpu.VMEM(square, BF16)] * 3,
        compiler_params=vmem(16),
        name="solve",
    )(nbr_weight, own, *received, deviation, centre)
    back = lax.all_to_all(
        analysis.reshape(128, 4, CELLS), "mem", split_axis=0, concat_axis=1, tiled=False,
        axis_index_groups=[ORDER],
    )
    return back.reshape(4, 65536)


def solution(mesh):
    in_specs = (P("mem", "grp"), P("mem", "grp"), P(("grp", "mem")), P(("grp", "mem")), P(), P())
    out_specs = P("mem", "grp")
    return jax.shard_map(shards, mesh=mesh, in_specs=in_specs, out_specs=out_specs, check_vma=False)
```

time: 118 us -> 103 us (0.87)
  starting transfers between devices: 31.3 us -> 18.1 us
  waiting for transfers between devices: 39.2 us -> 45.8 us
  Pallas kernels: 13.9 us -> 9.76 us
  local copies, waits for them, and re-layouts: 2.94 us -> 0.82 us
  blocking collectives: 29.8 us -> 27.8 us
    all_to_all x2 -> x1, waiting for transfers between devices: 28 us -> 39.8 us  [shards(): lax.all_to_all(both, 'mem', split_axis=0, concat_axis=0, tiled=False, axi...]
    all_to_all x2 -> x1, starting transfers between devices: 20.7 us -> 14 us  [shards(): lax.all_to_all(both, 'mem', split_axis=0, concat_axis=0, tiled=False, axi...]
    ppermute x4, starting transfers between devices: 9.86 us -> 3.43 us  [shards(): lax.ppermute(send, ('grp', 'mem'), swaps(by, parity))]
    ppermute x4, waiting for transfers between devices: 11.2 us -> 6 us  [shards(): lax.ppermute(send, ('grp', 'mem'), swaps(by, parity))]
    pallas_call x3 -> x4, Pallas kernels: 13.9 us -> 9.76 us  [the longest x1 5.36 us: shards(): pl.pallas_call(solve_kernel, out_shape=jax.ShapeDtypeStruct((64, 2, 4, CE...]
    unnamed x21 -> x9, local copies, waits for them, and re-layouts: 2.94 us -> 0.82 us
    all_to_all x1, blocking collectives: 29.8 us -> 27.8 us  [shards(): lax.all_to_all(analysis.reshape(128, 4, CELLS), 'mem', split_axis=0, conc...]
  transfers between devices with their start and end apart: 7 -> 6, of which waited for: 4 -> 3; matrix products, arithmetic and copies ran while one was open for 0% -> 0% of each run, Pallas kernels for 9% -> 0%
where the time goes in v1:
time: 103 us
  waiting for transfers between devices  45.8 us (44%)
  blocking collectives  27.8 us (27%)
  starting transfers between devices  18.1 us (18%)
  Pallas kernels  9.76 us (9%)
    all_to_all x1, waiting for transfers between devices, shards(): lax.all_to_all(both, 'mem', split_axis=0, concat_axis=0, tiled=False, axi...  39.8 us
    all_to_all x1, blocking collectives, shards(): lax.all_to_all(analysis.reshape(128, 4, CELLS), 'mem', split_axis=0, conc...  27.8 us
    all_to_all x1, starting transfers between devices, shards(): lax.all_to_all(both, 'mem', split_axis=0, concat_axis=0, tiled=False, axi...  14 us
    ppermute x4, waiting for transfers between devices, shards(): lax.ppermute(send, ('grp', 'mem'), swaps(by, parity))  6 us
    pallas_call x1, Pallas kernels, shards(): pl.pallas_call(solve_kernel, out_shape=jax.ShapeDtypeStruct((64, 2, 4, CE...  5.36 us
    ppermute x4, starting transfers between devices, shards(): lax.ppermute(send, ('grp', 'mem'), swaps(by, parity))  3.43 us
    pallas_call x1, Pallas kernels, shards(): pl.pallas_call(join_kernel, out_shape=pltpu.VMEM((128, 4, columns), BF16)...  2.52 us
  transfers between devices with their start and end apart: 6, of which 3 were waited for; matrix products, arithmetic and copies ran while one was open for 0% of the time, Pallas kernels for 0%

profile of v1, /device:TPU:1, one launch (start us, length us, event | category | flops | bytes accessed | tf_op | source)
XLA Modules:
  0.0 102.6 jit_solution(2508177723311534819)
XLA Ops:
  0.0 2.5 %join.1 = bf16[128,4,1536]{2,1,0:T(4,128)(2,1)} custom-call(bf16[128,4,1024]{2,1,0:T(4,128)(2,1)} %bitcast.21, bf16[128,4,512]{2,1,0:T(4,128)(2,1)} %bitcast.22), custom_call_target="tpu_custom_call" | custom-call | tf_op jit(solution)/shard_map/join/pallas_call | solution.py:229
  2.5 0.0 copy-start.3
  2.5 0.0 copy-start.1
  2.6 0.0 copy-start.2
  2.6 14.0 %all-to-all-start = ((bf16[128,4,1536]{2,1,0:T(4,128)(2,1)}), bf16[128,4,1536]{2,1,0:T(4,128)(2,1)S(1)}, u32[]{:S(2)}, u32[]{:S(2)}) async-start(bf16[128,4,1536]{2,1,0:T(4,128)(2,1)} %join.1), calls=%async_computation | async-start | bytes 3145728 | tf_op jit(solution)/shard_map/all_to_all | solution.py:241
  16.5 0.0 copy-done.3
  16.6 0.0 copy-done.1
  16.6 0.1 select_reduce_fusion
  16.7 0.0 copy-done.2
  16.7 0.7 collective-permute-start
  17.4 0.0 collective-permute-done.val_ref
  17.4 39.8 %all-to-all-done = bf16[128,4,1536]{2,1,0:T(4,128)(2,1)S(1)} async-done(((bf16[128,4,1536]{2,1,0:T(4,128)(2,1)}), bf16[128,4,1536]{2,1,0:T(4,128)(2,1)S(1)}, u32[]{:S(2)}, u32[]{:S(2)}) %all-to-all-start) | async-done | bytes 1572896 | tf_op jit(solution)/shard_map/all_to_all | solution.py:241
  57.2 0.0 copy-start
  57.2 1.5 %gram.1 = (f32[656,256]{1,0:T(8,128)S(1)}, bf16[656,256]{1,0:T(8,128)(2,1)S(1)}) custom-call(bf16[64,2,4,1536]{3,2,1,0:T(4,128)(2,1)S(1)} %bitcast.17, f32[2,1024]{1,0:T(2,128)S(1)} %collective-permute-done.val_ref), custom_call_target="tpu_custom_call" | custom-call | tf_op jit(solution)/shard_map/gram/pallas_call | solution.py:246
  58.7 0.4 collective-permute-start.1
  59.1 0.7 collective-permute-start.2
  59.8 2.2 %collective-permute-start.3 = (bf16[656,256]{1,0:T(8,128)(2,1)S(1)}, bf16[656,256]{1,0:T(8,128)(2,1)S(1)}, u32[]{:S(2)}, u32[]{:S(2)}) collective-permute-start(bf16[656,256]{1,0:T(8,128)(2,1)S(1)} %get-tuple-element.13), channel_id=1, source_target_pairs={{1,2},{2,1},{3,4},{4,3},{5,6},{6,5},{33,34},{34,33},{35,36},{36,35... | collective-permute-start | bytes 1007624 | tf_op jit(solution)/shard_map/ppermute | solution.py:259
  62.0 0.1 collective-permute-start.4
  62.1 0.4 state.1
  62.5 4.4 %collective-permute-done.1.ns0_ref = bf16[656,256]{1,0:T(8,128)(2,1)S(1)} collective-permute-done((bf16[656,256]{1,0:T(8,128)(2,1)S(1)}, bf16[656,256]{1,0:T(8,128)(2,1)S(1)}, u32[]{:S(2)}, u32[]{:S(2)}) %collective-permute-start.1) | collective-permute-done | bytes 335904 | tf_op jit(solution)/shard_map/ppermute | solution.py:259
  67.0 0.0 collective-permute-done.2.ns1_ref
  67.0 1.6 %collective-permute-done.3.ew1_ref = bf16[656,256]{1,0:T(8,128)(2,1)S(1)} collective-permute-done((bf16[656,256]{1,0:T(8,128)(2,1)S(1)}, bf16[656,256]{1,0:T(8,128)(2,1)S(1)}, u32[]{:S(2)}, u32[]{:S(2)}) %collective-permute-start.3) | collective-permute-done | bytes 335904 | tf_op jit(solution)/shard_map/ppermute | solution.py:259
  68.5 0.0 collective-permute-done.4.ew0_ref
  68.6 0.0 copy-done
  68.6 5.4 %solve.1 = bf16[64,2,4,512]{3,2,1,0:T(4,128)(2,1)S(1)} custom-call(f32[4]{0:T(128)S(1)} %copy-done, f32[656,256]{1,0:T(8,128)S(1)} %get-tuple-element.12.own_ref, bf16[656,256]{1,0:T(8,128)(2,1)S(1)} %collective-permute-done.1.ns0_ref, bf16[656,256]{1,0:T(8,128)(2,1)S(1)} %collective-permute-done.2.ns1_ref, ...), custom_call_target="tpu_custom_call" | custom-call | tf_op jit(solution)/shard_map/solve/pallas_call | solution.py:276
  73.9 27.8 %all_to_all.20 = bf16[128,4,1,512]{3,1,2,0:T(4,128)(2,1)S(1)} all-to-all(bf16[128,4,1,512]{3,1,2,0:T(4,128)(2,1)S(1)} %bitcast.19), channel_id=1, replica_groups={{0,1,2,3,4,5,6,7,32,33,34,35,36,37,38,39,64,65,66,67,68,69,70,71,96,97,..., dimensions={0} | all-to-all | bytes 1048576 | tf_op jit(solution)/shard_map/all_to_all | solution.py:285
  101.8 0.8 copy.11
  (2 shorter events, 0.0 us)
Async XLA Ops:
  2.5 14.0 %copy-start.3 = (bf16[16]{0:T(256)(128)(2,1)S(1)}, bf16[16]{0:T(256)(128)(2,1)}, u32[]{:S(2)}) copy-start(bf16[16]{0:T(256)(128)(2,1)} %param.10) | copy-start | bytes 100
  2.5 14.0 %copy-start.1 = (s32[1024]{0:T(1024)S(1)}, s32[1024]{0:T(1024)}, u32[]{:S(2)}) copy-start(s32[1024]{0:T(1024)} %param.9) | copy-start | bytes 12292
  2.6 14.1 %copy-start.2 = (f32[1024]{0:T(1024)S(1)}, f32[1024]{0:T(1024)}, u32[]{:S(2)}) copy-start(f32[1024]{0:T(1024)} %param.8) | copy-start | bytes 12292
  2.6 54.6 %all-to-all-start = ((bf16[128,4,1536]{2,1,0:T(4,128)(2,1)}), bf16[128,4,1536]{2,1,0:T(4,128)(2,1)S(1)}, u32[]{:S(2)}, u32[]{:S(2)}) async-start(bf16[128,4,1536]{2,1,0:T(4,128)(2,1)} %join.1), calls=%async_computation | async-start | bytes 3145728 | tf_op jit(solution)/shard_map/all_to_all | solution.py:241
  16.7 0.7 collective-permute-start
  57.2 11.4 %copy-start = (f32[4]{0:T(128)S(1)}, f32[4]{0:T(128)}, u32[]{:S(2)}) copy-start(f32[4]{0:T(128)} %weight_ref.1) | copy-start | bytes 52
  58.7 8.3 %collective-permute-start.1 = (bf16[656,256]{1,0:T(8,128)(2,1)S(1)}, bf16[656,256]{1,0:T(8,128)(2,1)S(1)}, u32[]{:S(2)}, u32[]{:S(2)}) collective-permute-start(bf16[656,256]{1,0:T(8,128)(2,1)S(1)} %get-tuple-element.13), channel_id=1, source_target_pairs={{0,32},{32,0},{1,33},{33,1},{2,34},{34,2},{3,35},{35,3},{4,36},{36... | collective-permute-start | bytes 1007624 | tf_op jit(solution)/shard_map/ppermute | solution.py:259
  59.1 7.9 %collective-permute-start.2 = (bf16[656,256]{1,0:T(8,128)(2,1)S(1)}, bf16[656,256]{1,0:T(8,128)(2,1)S(1)}, u32[]{:S(2)}, u32[]{:S(2)}) collective-permute-start(bf16[656,256]{1,0:T(8,128)(2,1)S(1)} %get-tuple-element.13), channel_id=1, source_target_pairs={{32,64},{64,32},{33,65},{65,33},{34,66},{66,34},{35,67},{67,35},{3... | collective-permute-start | bytes 1007624 | tf_op jit(solution)/shard_map/ppermute | solution.py:259
  59.8 8.8 %collective-permute-start.3 = (bf16[656,256]{1,0:T(8,128)(2,1)S(1)}, bf16[656,256]{1,0:T(8,128)(2,1)S(1)}, u32[]{:S(2)}, u32[]{:S(2)}) collective-permute-start(bf16[656,256]{1,0:T(8,128)(2,1)S(1)} %get-tuple-element.13), channel_id=1, source_target_pairs={{1,2},{2,1},{3,4},{4,3},{5,6},{6,5},{33,34},{34,33},{35,36},{36,35... | collective-permute-start | bytes 1007624 | tf_op jit(solution)/shard_map/ppermute | solution.py:259
  62.0 6.5 %collective-permute-start.4 = (bf16[656,256]{1,0:T(8,128)(2,1)S(1)}, bf16[656,256]{1,0:T(8,128)(2,1)S(1)}, u32[]{:S(2)}, u32[]{:S(2)}) collective-permute-start(bf16[656,256]{1,0:T(8,128)(2,1)S(1)} %get-tuple-element.13), channel_id=1, source_target_pairs={{0,1},{1,0},{2,3},{3,2},{4,5},{5,4},{6,7},{7,6},{32,33},{33,32},{3... | collective-permute-start | bytes 1007624 | tf_op jit(solution)/shard_map/ppermute | solution.py:259

commit v2 on v1

--- a/solution.py
+++ b/solution.py
@@ -6,15 +6,15 @@
 from jax.sharding import PartitionSpec as P
 
 MEMBERS = 512
-SWEEPS = 5
 CELLS = 512
 LOCAL_OBS = 1024
+JOINED = 16
+STORES = 4
 ROW_PATCHES = 8
 HALF = MEMBERS // 2
 QUARTER = MEMBERS // 4
 VEC = 16
-TAIL = MEMBERS + QUARTER
-PACKED = TAIL + VEC
+PACKED = MEMBERS + VEC
 F32 = jnp.float32
 BF16 = jnp.bfloat16
 
@@ -23,7 +23,7 @@
     order = []
     for row in range(16):
         z, step = row // 4, row % 4
-        x = step if z % 2 == 0 else 3 - step
+        x = 3 - step if z % 2 == 0 else step
         order += [x * 32 + z * 8 + w for w in range(ROW_PATCHES)]
     return order
 
@@ -49,7 +49,7 @@
 def swap_weights(weight_ref):
     west, east, north, south = (weight_ref[k] for k in range(4))
     mem = lax.axis_index("mem")
-    even_row = lax.rem(lax.div(mem, 32) + lax.div(mem, 8), 2) == 0
+    even_row = lax.rem(lax.div(mem, 32) + lax.div(mem, 8), 2) == 1
     even_column = lax.rem(mem, 2) == 0
     return (
         jnp.where(even_row, south, north),
@@ -65,15 +65,33 @@
     return jnp.sum(picked, axis=0)
 
 
-def join_kernel(obs_ref, state_ref, out_ref, sem):
-    copies = [
-        pltpu.make_async_copy(obs_ref, out_ref.at[:, :, pl.ds(0, LOCAL_OBS)], sem.at[0]),
-        pltpu.make_async_copy(state_ref, out_ref.at[:, :, pl.ds(LOCAL_OBS, CELLS)], sem.at[1]),
-    ]
-    for copy in copies:
-        copy.start()
-    for copy in copies:
-        copy.wait()
+def join_kernel(obs_ref, state_ref, out_ref, both_ref, in_sem, out_sem):
+    def chunk(k):
+        return pl.ds(k * JOINED, JOINED)
+
+    def fetch(k):
+        at = chunk(k)
+        return (
+            pltpu.make_async_copy(
+                obs_ref.at[at], both_ref.at[at, :, pl.ds(0, LOCAL_OBS)], in_sem.at[0, k]
+            ),
+            pltpu.make_async_copy(
+                state_ref.at[at], both_ref.at[at, :, pl.ds(LOCAL_OBS, CELLS)], in_sem.at[1, k]
+            ),
+        )
+
+    def put(k):
+        return pltpu.make_async_copy(both_ref.at[chunk(k)], out_ref.at[chunk(k)], out_sem.at[k])
+
+    for k in range(128 // JOINED):
+        for copy in fetch(k):
+            copy.start()
+    for k in range(128 // JOINED):
+        for copy in fetch(k):
+            copy.wait()
+        put(k).start()
+    for k in range(128 // JOINED):
+        put(k).wait()
 
 
 def gather_rows(ref, columns, rows_ref):
@@ -111,25 +129,33 @@
     second = lax.dot_general(
         left_ref[HALF:], spread_ref[HALF:MEMBERS], contract, preferred_element_type=F32
     )
-    for at, part in (
-        ((slice(0, QUARTER), slice(0, QUARTER)), first[0:QUARTER, 0:QUARTER]),
-        ((slice(0, QUARTER), slice(QUARTER, HALF)), second[0:QUARTER, 0:QUARTER]),
-        ((slice(QUARTER, MEMBERS), slice(0, HALF)), first[QUARTER:MEMBERS]),
-        ((slice(MEMBERS, TAIL), slice(0, HALF)), second[QUARTER:HALF]),
-    ):
-        own_ref[at] = part
-        send_ref[at] = part.astype(BF16)
+    row = lax.broadcasted_iota(jnp.int32, (QUARTER, QUARTER), 0)
+    col = lax.broadcasted_iota(jnp.int32, (QUARTER, QUARTER), 1)
+
+    def put(rows, columns, part):
+        own_ref[rows, columns] = part
+        send_ref[rows, columns] = part.astype(BF16)
+
+    low, high = slice(0, QUARTER), slice(QUARTER, HALF)
+    diagonals = []
+    for part, columns in ((first, low), (second, high)):
+        last = part[high, high]
+        put(low, columns, jnp.where(row >= col, part[low, low], last.T))
+        put(high, columns, part[high, low])
+        diagonals.append(jnp.sum(jnp.where(row == col, last, 0.0), axis=0, keepdims=True))
+    put(slice(HALF, MEMBERS), slice(0, HALF), first[HALF:MEMBERS])
     row = lax.broadcasted_iota(jnp.int32, (VEC, HALF), 0)
-    vec = jnp.where(row < 8, first[MEMBERS:], second[HALF:])
-    high = vec.astype(BF16).astype(F32)
+    tail = jnp.where(row < 8, first[MEMBERS:], second[HALF:])
+    tail = jnp.where(row % 4 == 2, jnp.concatenate(diagonals, axis=1), tail)
+    rounded = tail.astype(BF16).astype(F32)
     is_high = row % 8 < 4
-    own_ref[TAIL:PACKED] = jnp.where(is_high, vec, 0.0)
-    send_ref[TAIL:PACKED] = jnp.where(is_high, high, vec - high).astype(BF16)
+    own_ref[MEMBERS:] = jnp.where(is_high, tail, 0.0)
+    send_ref[MEMBERS:] = jnp.where(is_high, rounded, tail - rounded).astype(BF16)
 
 
 def solve_kernel(
     weight_ref, own_ref, ns0_ref, ns1_ref, ew1_ref, ew0_ref, dev_ref, centre_ref, out_ref,
-    sys_ref, t_ref, w_ref, t2_ref, tb_ref, wb_ref, t2b_ref,
+    sys_ref, t_ref, w_ref, w2_ref, tb_ref, wb_ref, w2b_ref, sb_ref, ub_ref,
 ):
     weights = swap_weights(weight_ref)
 
@@ -143,54 +169,56 @@
     row = lax.broadcasted_iota(jnp.int32, (QUARTER, QUARTER), 0)
     col = lax.broadcasted_iota(jnp.int32, (QUARTER, QUARTER), 1)
 
-    def diagonal(block):
-        block = jnp.where(row >= col, block, block.T)
-        return block + jnp.where(row == col, MEMBERS - 1.0, 0.0)
-
-    top = total(0, QUARTER)
-    for start, left, at in ((0, 0, QUARTER), (HALF, QUARTER, MEMBERS)):
+    top, low, tail = total(0, QUARTER), total(QUARTER, QUARTER), total(MEMBERS, VEC)
+    inflation = jnp.where(row == col, MEMBERS - 1.0, 0.0)
+    diagonals = tail[2:3] + tail[6:7]
+    for start, columns in ((0, slice(0, QUARTER)), (HALF, slice(QUARTER, HALF))):
         a, b, c = start, start + QUARTER, start + HALF
-        low = total(at, QUARTER)
-        sys_ref[a:b, a:b] = diagonal(top[:, left:left + QUARTER])
-        sys_ref[b:c, a:b] = low[:, 0:QUARTER]
-        sys_ref[a:b, b:c] = low[:, 0:QUARTER].T
-        sys_ref[b:c, b:c] = diagonal(low[:, QUARTER:])
+        square, cross = top[:, columns], low[:, columns]
+        turned = square.T
+        sys_ref[a:b, a:b] = jnp.where(row >= col, square, turned) + inflation
+        square = jnp.where(row < col, square, turned)
+        sys_ref[b:c, b:c] = jnp.where(row == col, diagonals[:, columns], square) + inflation
+        sys_ref[b:c, a:b] = cross
+        sys_ref[a:b, b:c] = cross.T
     cross = total(HALF, HALF)
     sys_ref[HALF:MEMBERS, 0:HALF] = cross
     sys_ref[0:HALF, HALF:MEMBERS] = cross.T
-    vec = total(TAIL, VEC)
-    rhs = jnp.concatenate([vec[0:1] + vec[4:5], vec[8:9] + vec[12:13]], axis=1)
+    rhs = jnp.concatenate([tail[0:1] + tail[4:5], tail[8:9] + tail[12:13]], axis=1)
 
     system = sys_ref[...]
-    norm = jnp.sqrt(jnp.sum(jnp.sum(system * system, axis=0, keepdims=True), axis=1, keepdims=True))
-    t = system / norm
+    squares = jnp.sum(jnp.sum(system * system, axis=0, keepdims=True), axis=1, keepdims=True)
+    norm = jnp.sqrt(squares)
+
+    def dot(a, b):
+        return jnp.dot(a[...], b[...], preferred_element_type=F32)
+
+    def two_sweeps(w_ref, wb_ref):
+        square = dot(tb_ref, tb_ref)
+        sb_ref[...] = square.astype(BF16)
+        ub_ref[...] = (0.0625 * square - 0.5625 * t_ref[...]).astype(BF16)
+        w_ref[...] = 1.6875 * square - 2.4375 * t_ref[...]
+        w = w_ref[...] + dot(ub_ref, sb_ref)
+        w_ref[...] = w
+        wb_ref[...] = w.astype(BF16)
+        ub_ref[...] = (4.5 * w_ref[...] + dot(wb_ref, wb_ref)).astype(BF16)
+        t = 5.0625 * t_ref[...] + dot(ub_ref, tb_ref)
+        t_ref[...] = t
+        tb_ref[...] = t.astype(BF16)
+
+    t = system * (1.0 / norm)
     t_ref[...] = t
     tb_ref[...] = t.astype(BF16)
-
-    def dot(a, b):
-        return jnp.dot(a[...], b[...], preferred_element_type=F32)
-
-    scale = 1.0
-    for sweep in range(SWEEPS):
-        last = sweep == SWEEPS - 1
-        if sweep == 0:
-            w = -0.5 * t_ref[...]
-        else:
-            w = 1.5 * w_ref[...] - (0.5 * scale) * t_ref[...] - 0.5 * dot(tb_ref, wb_ref)
-        scale *= 1.5
-        w_ref[...] = w
-        if not last:
-            wb_ref[...] = w.astype(BF16)
-            t2 = dot(tb_ref, tb_ref)
-            t2_ref[...] = t2
-            t2b_ref[...] = t2.astype(BF16)
-            t = 2.25 * t_ref[...] - 1.5 * t2_ref[...] + 0.25 * dot(t2b_ref, tb_ref)
-            t_ref[...] = t
-            tb_ref[...] = t.astype(BF16)
+    two_sweeps(w_ref, wb_ref)
+    two_sweeps(w2_ref, w2b_ref)
+    w = 2.25 * (w_ref[...] + w2_ref[...]) + dot(wb_ref, w2b_ref)
+    w_ref[...] = w
+    wb_ref[...] = w.astype(BF16)
+    w = 1.5 * w_ref[...] - 2.53125 * t_ref[...] - 0.5 * dot(wb_ref, tb_ref)
 
     row = lax.broadcasted_iota(jnp.int32, (MEMBERS, MEMBERS), 0)
     col = lax.broadcasted_iota(jnp.int32, (MEMBERS, MEMBERS), 1)
-    root_inv = w_ref[...] + jnp.where(row == col, scale, 0.0)
+    root_inv = w + jnp.where(row == col, 1.5 * 5.0625, 0.0)
     half_step = jnp.sum(root_inv * rhs, axis=1, keepdims=True)
     mean_weight = jnp.sum(root_inv * half_step, axis=0, keepdims=True) / norm
     tb_ref[...] = (jnp.sqrt((MEMBERS - 1.0) / norm) * root_inv + mean_weight).astype(BF16)
@@ -199,6 +227,18 @@
     out_ref[:, 1] = analysis[:, 4:8].astype(BF16)
 
 
+def store_kernel(in_ref, out_ref, sem):
+    width = in_ref.shape[1] // STORES
+    copies = []
+    for k in range(STORES):
+        at = pl.ds(k * width, width)
+        copies.append(pltpu.make_async_copy(in_ref.at[:, at], out_ref.at[:, at], sem.at[k]))
+    for copy in copies:
+        copy.start()
+    for copy in copies:
+        copy.wait()
+
+
 def state_kernel(state_ref, dev_ref, centre_ref):
     centre = gather_rows(state_ref, pl.ds(LOCAL_OBS, CELLS), dev_ref)
     centre_ref[...] = centre
@@ -228,11 +268,15 @@
     columns = LOCAL_OBS + CELLS
     both = pl.pallas_call(
         join_kernel,
-        out_shape=pltpu.VMEM((128, 4, columns), BF16),
+        out_shape=jax.ShapeDtypeStruct((128, 4, columns), BF16),
         in_specs=[HBM, HBM],
-        out_specs=VMEM,
-        scratch_shapes=[pltpu.SemaphoreType.DMA((2,))],
-        compiler_params=vmem(2),
+        out_specs=HBM,
+        scratch_shapes=[
+            pltpu.VMEM((128, 4, columns), BF16),
+            pltpu.SemaphoreType.DMA((2, 128 // JOINED)),
+            pltpu.SemaphoreType.DMA((128 // JOINED,)),
+        ],
+        compiler_params=vmem(4),
         name="join",
     )(
         in_hbm(obs_ens.reshape(4, 128, LOCAL_OBS).transpose(1, 0, 2)),
@@ -246,8 +290,8 @@
     own, send = pl.pallas_call(
         gram_kernel,
         out_shape=(
-            pltpu.VMEM((PACKED, HALF), F32),
-            pltpu.VMEM((PACKED, HALF), BF16),
+            jax.ShapeDtypeStruct((PACKED, HALF), F32),
+            jax.ShapeDtypeStruct((PACKED, HALF), BF16),
         ),
         in_specs=[VMEM, VMEM],
         out_specs=(VMEM, VMEM),
@@ -278,7 +322,7 @@
         out_shape=jax.ShapeDtypeStruct((64, 2, 4, CELLS), BF16),
         in_specs=[SMEM] + [VMEM] * 7,
         out_specs=VMEM,
-        scratch_shapes=[pltpu.VMEM(square, F32)] * 4 + [pltpu.VMEM(square, BF16)] * 3,
+        scratch_shapes=[pltpu.VMEM(square, F32)] * 4 + [pltpu.VMEM(square, BF16)] * 5,
         compiler_params=vmem(16),
         name="solve",
     )(nbr_weight, own, *received, deviation, centre)
@@ -286,7 +330,15 @@
         analysis.reshape(128, 4, CELLS), "mem", split_axis=0, concat_axis=1, tiled=False,
         axis_index_groups=[ORDER],
     )
-    return back.reshape(4, 65536)
+    return pl.pallas_call(
+        store_kernel,
+        out_shape=jax.ShapeDtypeStruct((4, 65536), BF16),
+        in_specs=[VMEM],
+        out_specs=HBM,
+        scratch_shapes=[pltpu.SemaphoreType.DMA((STORES,))],
+        compiler_params=vmem(2),
+        name="store",
+    )(back.reshape(4, 65536))
 
 
 def solution(mesh):

time: 103 us -> 101 us (0.981)
  waiting for transfers between devices: 45.8 us -> 40.8 us
  starting transfers between devices: 18.1 us -> 22.5 us
    all_to_all x1, waiting for transfers between devices: 39.8 us -> 9.96 us  [shards(): lax.all_to_all(both, 'mem', split_axis=0, concat_axis=0, tiled=False, axi...]
    ppermute x1, waiting for transfers between devices: 0.01 us -> 26.8 us  [shards(): lax.ppermute(values, ('grp', 'mem'), [(p, device_of(p)) for p in range(25...]
    ppermute x4, starting transfers between devices: 3.43 us -> 5.73 us  [shards(): lax.ppermute(send, ('grp', 'mem'), swaps(by, parity))]
    ppermute x4, waiting for transfers between devices: 6 us -> 4.04 us  [shards(): lax.ppermute(send, ('grp', 'mem'), swaps(by, parity))]
    ppermute x1, starting transfers between devices: 0.66 us -> 1.97 us  [shards(): lax.ppermute(values, ('grp', 'mem'), [(p, device_of(p)) for p in range(25...]
    pallas_call x2 -> x3, Pallas kernels: 3.98 us -> 4.71 us  [the longest x1 2.37 us: shards(): pl.pallas_call(join_kernel, out_shape=jax.ShapeDtypeStruct((128, 4, colum...]
  transfers between devices with their start and end apart: 6 -> 6, of which waited for: 3 -> 5; matrix products, arithmetic and copies ran while one was open for 0% -> 0% of each run, Pallas kernels for 0% -> 0%
where the time goes in v2:
time: 101 us
  waiting for transfers between devices  40.8 us (40%)
  blocking collectives  27.1 us (27%)
  starting transfers between devices  22.5 us (22%)
  Pallas kernels  10.1 us (10%)
    all_to_all x1, blocking collectives, shards(): lax.all_to_all(analysis.reshape(128, 4, CELLS), 'mem', split_axis=0, conc...  27.1 us
    ppermute x1, waiting for transfers between devices, shards(): lax.ppermute(values, ('grp', 'mem'), [(p, device_of(p)) for p in range(25...  26.8 us
    all_to_all x1, starting transfers between devices, shards(): lax.all_to_all(both, 'mem', split_axis=0, concat_axis=0, tiled=False, axi...  14.8 us
    all_to_all x1, waiting for transfers between devices, shards(): lax.all_to_all(both, 'mem', split_axis=0, concat_axis=0, tiled=False, axi...  9.96 us
    ppermute x4, starting transfers between devices, shards(): lax.ppermute(send, ('grp', 'mem'), swaps(by, parity))  5.73 us
    pallas_call x1, Pallas kernels, shards(): pl.pallas_call(solve_kernel, out_shape=jax.ShapeDtypeStruct((64, 2, 4, CE...  4.99 us
    ppermute x4, waiting for transfers between devices, shards(): lax.ppermute(send, ('grp', 'mem'), swaps(by, parity))  4.04 us
    pallas_call x1, Pallas kernels, shards(): pl.pallas_call(join_kernel, out_shape=jax.ShapeDtypeStruct((128, 4, colum...  2.37 us
  transfers between devices with their start and end apart: 6, of which 5 were waited for; matrix products, arithmetic and copies ran while one was open for 0% of the time, Pallas kernels for 0%

profile of v2, /device:TPU:1, one launch (start us, length us, event | category | flops | bytes accessed | tf_op | source)
XLA Modules:
  0.0 100.8 jit_solution(18325052764619209251)
XLA Ops:
  0.0 2.4 %join.1 = bf16[128,4,1536]{2,1,0:T(4,128)(2,1)} custom-call(bf16[128,4,1024]{2,1,0:T(4,128)(2,1)} %bitcast.21, bf16[128,4,512]{2,1,0:T(4,128)(2,1)} %bitcast.22), custom_call_target="tpu_custom_call" | custom-call | tf_op jit(solution)/shard_map/join/pallas_call | solution.py:269
  2.4 0.0 copy-start.3
  2.4 0.0 copy-start.1
  2.4 0.0 copy-start.2
  2.4 14.8 %all-to-all-start = ((bf16[128,4,1536]{2,1,0:T(4,128)(2,1)}), bf16[128,4,1536]{2,1,0:T(4,128)(2,1)S(1)}, u32[]{:S(2)}, u32[]{:S(2)}) async-start(bf16[128,4,1536]{2,1,0:T(4,128)(2,1)} %join.1), calls=%async_computation | async-start | bytes 3145728 | tf_op jit(solution)/shard_map/all_to_all | solution.py:285
  17.2 0.0 copy-done.3
  17.2 0.0 copy-done.1
  17.2 0.1 select_reduce_fusion
  17.3 0.0 copy-done.2
  17.3 2.0 %collective-permute-start = (f32[2,1024]{1,0:T(2,128)S(1)}, f32[2,1024]{1,0:T(2,128)S(1)}, u32[]{:S(2)}, u32[]{:S(2)}) collective-permute-start(f32[2,1024]{1,0:T(2,128)S(1)} %pad_maximum_fusion), channel_id=1, source_target_pairs={{0,96},{1,97},{2,98},{3,99},{4,100},{5,101},{6,102},{7,103},{8,64}... | collective-permute-start | bytes 24584 | tf_op jit(solution)/shard_map/ppermute | solution.py:289
  19.3 26.8 %collective-permute-done.val_ref = f32[2,1024]{1,0:T(2,128)S(1)} collective-permute-done((f32[2,1024]{1,0:T(2,128)S(1)}, f32[2,1024]{1,0:T(2,128)S(1)}, u32[]{:S(2)}, u32[]{:S(2)}) %collective-permute-start) | collective-permute-done | bytes 8224 | tf_op jit(solution)/shard_map/ppermute | solution.py:289
  46.1 10.0 %all-to-all-done = bf16[128,4,1536]{2,1,0:T(4,128)(2,1)S(1)} async-done(((bf16[128,4,1536]{2,1,0:T(4,128)(2,1)}), bf16[128,4,1536]{2,1,0:T(4,128)(2,1)S(1)}, u32[]{:S(2)}, u32[]{:S(2)}) %all-to-all-start) | async-done | bytes 1572896 | tf_op jit(solution)/shard_map/all_to_all | solution.py:285
  56.1 0.0 copy-start
  56.1 1.5 %gram.1 = (f32[528,256]{1,0:T(8,128)S(1)}, bf16[528,256]{1,0:T(8,128)(2,1)S(1)}) custom-call(bf16[64,2,4,1536]{3,2,1,0:T(4,128)(2,1)S(1)} %bitcast.17, f32[2,1024]{1,0:T(2,128)S(1)} %collective-permute-done.val_ref), custom_call_target="tpu_custom_call" | custom-call | tf_op jit(solution)/shard_map/gram/pallas_call | solution.py:290
  57.6 0.2 collective-permute-start.1
  57.8 1.9 %collective-permute-start.2 = (bf16[528,256]{1,0:T(8,128)(2,1)S(1)}, bf16[528,256]{1,0:T(8,128)(2,1)S(1)}, u32[]{:S(2)}, u32[]{:S(2)}) collective-permute-start(bf16[528,256]{1,0:T(8,128)(2,1)S(1)} %get-tuple-element.13), channel_id=1, source_target_pairs={{64,32},{32,64},{65,33},{33,65},{66,34},{34,66},{67,35},{35,67},{6... | collective-permute-start | bytes 811016 | tf_op jit(solution)/shard_map/ppermute | solution.py:303
  59.8 3.5 %collective-permute-start.3 = (bf16[528,256]{1,0:T(8,128)(2,1)S(1)}, bf16[528,256]{1,0:T(8,128)(2,1)S(1)}, u32[]{:S(2)}, u32[]{:S(2)}) collective-permute-start(bf16[528,256]{1,0:T(8,128)(2,1)S(1)} %get-tuple-element.13), channel_id=1, source_target_pairs={{97,98},{98,97},{99,100},{100,99},{101,102},{102,101},{65,66},{66,... | collective-permute-start | bytes 811016 | tf_op jit(solution)/shard_map/ppermute | solution.py:303
  63.3 0.1 collective-permute-start.4
  63.4 0.4 state.1
  63.8 1.6 %collective-permute-done.1.ns0_ref = bf16[528,256]{1,0:T(8,128)(2,1)S(1)} collective-permute-done((bf16[528,256]{1,0:T(8,128)(2,1)S(1)}, bf16[528,256]{1,0:T(8,128)(2,1)S(1)}, u32[]{:S(2)}, u32[]{:S(2)}) %collective-permute-start.1) | collective-permute-done | bytes 270368 | tf_op jit(solution)/shard_map/ppermute | solution.py:303
  65.4 1.8 %collective-permute-done.2.ns1_ref = bf16[528,256]{1,0:T(8,128)(2,1)S(1)} collective-permute-done((bf16[528,256]{1,0:T(8,128)(2,1)S(1)}, bf16[528,256]{1,0:T(8,128)(2,1)S(1)}, u32[]{:S(2)}, u32[]{:S(2)}) %collective-permute-start.2) | collective-permute-done | bytes 270368 | tf_op jit(solution)/shard_map/ppermute | solution.py:303
  67.2 0.6 collective-permute-done.3.ew1_ref
  67.8 0.0 collective-permute-done.4.ew0_ref
  67.8 0.0 copy-done
  67.8 5.0 %solve.1 = bf16[64,2,4,512]{3,2,1,0:T(4,128)(2,1)S(1)} custom-call(f32[4]{0:T(128)S(1)} %copy-done, f32[528,256]{1,0:T(8,128)S(1)} %get-tuple-element.12.own_ref, bf16[528,256]{1,0:T(8,128)(2,1)S(1)} %collective-permute-done.1.ns0_ref, bf16[528,256]{1,0:T(8,128)(2,1)S(1)} %collective-permute-done.2.ns1_ref, ...), custom_call_target="tpu_custom_call" | custom-call | tf_op jit(solution)/shard_map/solve/pallas_call | solution.py:320
  72.8 27.1 %all_to_all.20 = bf16[128,4,1,512]{3,1,2,0:T(4,128)(2,1)S(1)} all-to-all(bf16[128,4,1,512]{3,1,2,0:T(4,128)(2,1)S(1)} %bitcast.19), channel_id=1, replica_groups={{96,97,98,99,100,101,102,103,64,65,66,67,68,69,70,71,32,33,34,35,36,37,..., dimensions={0} | all-to-all | bytes 1048576 | tf_op jit(solution)/shard_map/all_to_all | solution.py:329
  99.9 0.8 store.1
  (2 shorter events, 0.0 us)
Async XLA Ops:
  2.4 14.8 %copy-start.3 = (bf16[16]{0:T(256)(128)(2,1)S(1)}, bf16[16]{0:T(256)(128)(2,1)}, u32[]{:S(2)}) copy-start(bf16[16]{0:T(256)(128)(2,1)} %param.10) | copy-start | bytes 100
  2.4 14.8 %copy-start.1 = (s32[1024]{0:T(1024)S(1)}, s32[1024]{0:T(1024)}, u32[]{:S(2)}) copy-start(s32[1024]{0:T(1024)} %param.9) | copy-start | bytes 12292
  2.4 14.9 %copy-start.2 = (f32[1024]{0:T(1024)S(1)}, f32[1024]{0:T(1024)}, u32[]{:S(2)}) copy-start(f32[1024]{0:T(1024)} %param.8) | copy-start | bytes 12292
  2.4 53.7 %all-to-all-start = ((bf16[128,4,1536]{2,1,0:T(4,128)(2,1)}), bf16[128,4,1536]{2,1,0:T(4,128)(2,1)S(1)}, u32[]{:S(2)}, u32[]{:S(2)}) async-start(bf16[128,4,1536]{2,1,0:T(4,128)(2,1)} %join.1), calls=%async_computation | async-start | bytes 3145728 | tf_op jit(solution)/shard_map/all_to_all | solution.py:285
  17.3 28.8 %collective-permute-start = (f32[2,1024]{1,0:T(2,128)S(1)}, f32[2,1024]{1,0:T(2,128)S(1)}, u32[]{:S(2)}, u32[]{:S(2)}) collective-permute-start(f32[2,1024]{1,0:T(2,128)S(1)} %pad_maximum_fusion), channel_id=1, source_target_pairs={{0,96},{1,97},{2,98},{3,99},{4,100},{5,101},{6,102},{7,103},{8,64}... | collective-permute-start | bytes 24584 | tf_op jit(solution)/shard_map/ppermute | solution.py:289
  56.1 11.8 %copy-start = (f32[4]{0:T(128)S(1)}, f32[4]{0:T(128)}, u32[]{:S(2)}) copy-start(f32[4]{0:T(128)} %weight_ref.1) | copy-start | bytes 52
  57.6 7.8 %collective-permute-start.1 = (bf16[528,256]{1,0:T(8,128)(2,1)S(1)}, bf16[528,256]{1,0:T(8,128)(2,1)S(1)}, u32[]{:S(2)}, u32[]{:S(2)}) collective-permute-start(bf16[528,256]{1,0:T(8,128)(2,1)S(1)} %get-tuple-element.13), channel_id=1, source_target_pairs={{96,64},{64,96},{97,65},{65,97},{98,66},{66,98},{99,67},{67,99},{1... | collective-permute-start | bytes 811016 | tf_op jit(solution)/shard_map/ppermute | solution.py:303
  57.8 9.4 %collective-permute-start.2 = (bf16[528,256]{1,0:T(8,128)(2,1)S(1)}, bf16[528,256]{1,0:T(8,128)(2,1)S(1)}, u32[]{:S(2)}, u32[]{:S(2)}) collective-permute-start(bf16[528,256]{1,0:T(8,128)(2,1)S(1)} %get-tuple-element.13), channel_id=1, source_target_pairs={{64,32},{32,64},{65,33},{33,65},{66,34},{34,66},{67,35},{35,67},{6... | collective-permute-start | bytes 811016 | tf_op jit(solution)/shard_map/ppermute | solution.py:303
  59.8 8.1 %collective-permute-start.3 = (bf16[528,256]{1,0:T(8,128)(2,1)S(1)}, bf16[528,256]{1,0:T(8,128)(2,1)S(1)}, u32[]{:S(2)}, u32[]{:S(2)}) collective-permute-start(bf16[528,256]{1,0:T(8,128)(2,1)S(1)} %get-tuple-element.13), channel_id=1, source_target_pairs={{97,98},{98,97},{99,100},{100,99},{101,102},{102,101},{65,66},{66,... | collective-permute-start | bytes 811016 | tf_op jit(solution)/shard_map/ppermute | solution.py:303
  63.3 4.6 %collective-permute-start.4 = (bf16[528,256]{1,0:T(8,128)(2,1)S(1)}, bf16[528,256]{1,0:T(8,128)(2,1)S(1)}, u32[]{:S(2)}, u32[]{:S(2)}) collective-permute-start(bf16[528,256]{1,0:T(8,128)(2,1)S(1)} %get-tuple-element.13), channel_id=1, source_target_pairs={{96,97},{97,96},{98,99},{99,98},{100,101},{101,100},{102,103},{103... | collective-permute-start | bytes 811016 | tf_op jit(solution)/shard_map/ppermute | solution.py:303
